TPU v7x, 32 devices: a whole 2x2x4 slice. The times are simulated.
32 devices in a mesh: group: 2 (over y), ctx: 8 (over z, x), tp: 2 (over core).
Axes of the slice: x: 2, y: 2, z: 4, core: 2. Of those that a mesh axis runs over, the one named last changes fastest.
Arguments:
- hidden: bfloat16 [256, 16384], P(('group', 'ctx')), parts along dimension 0, may hold values from -6 to 6
- q_base: bfloat16 [256, 8192], P(('group', 'ctx'), 'tp'), parts along dimension 0, may hold values from -6 to 6
- adapter_down: bfloat16 [16, 16384, 64], P(('group', 'ctx')), parts along dimension 0, may hold values from -0.046875 to 0.046875
- adapter_up: bfloat16 [16, 64, 8192], P(('group', 'ctx'), None, 'tp'), parts along dimension 0, may hold values from -0.75 to 0.75
- adapter_owner: int32 [2], P('group'), parts along dimension 0, may hold values from 0 to 7
- turn_start: int32 [2], P('group'), parts along dimension 0, may hold values from 512 to 2047
- shard_lengths: int32 [16], P('group'), parts along dimension 0, may hold values from 1 to 64, 384 in all
- stored_keys: bfloat16 [1024, 512], P(('group', 'ctx'), 'tp'), parts along dimension 0, may hold values from -250 to 250
- stored_values: bfloat16 [1024, 512], P(('group', 'ctx'), 'tp'), parts along dimension 0, may hold values from -6 to 6
- unrotated_turn_keys: bfloat16 [256, 512], P(('group', 'ctx'), 'tp'), parts along dimension 0, may hold values from -15 to 15
- incoming_values: bfloat16 [256, 512], P(('group', 'ctx'), 'tp'), parts along dimension 0, may hold values from -6 to 6
Outputs:
- attended: bfloat16 [256, 8192], P(('group', 'ctx'), 'tp'), parts along dimension 0
There are 2 independent parts, one for each index of `group`. A program takes and returns all parts, laid end to end along the dimension named above; each array names one. Nothing has to cross between parts.
Inputs may be any that keep to these rules, and one draw needn't show every extreme that they name: The used slots of shard s are its slots 0 .. shard_lengths[s] - 1; some shard uses all 64.
All inputs are finite; a program needn't handle non-finite values.
Results may differ from a plain program's by a relative error of at most 0.019.
The roundings to bfloat16 on the way count: a program that leaves them out, or rounds other values in their place, can miss the bound.
Values may be sent and summed in bfloat16 or wider, within the bound.
No kernel may reach another device: no remote copies, remote signals or barrier semaphores. Data moves between devices by JAX's collectives and lax.ppermute only.
A program may use at most 64 MiB of HBM per device.

v0:
```python
import math
import jax
import jax.numpy as jnp
from jax import lax
from jax.sharding import PartitionSpec as P

HEAD_SIZE = 128


def spread(shard, axis, root):
    mine = lax.axis_index(axis) == root
    return lax.psum(jnp.where(mine, shard, jnp.zeros_like(shard)), axis)


def apply_rotary(values, token_positions, heads):
    half_dim = HEAD_SIZE // 2
    inverse = jnp.exp(
        jnp.arange(half_dim, dtype=jnp.float32) * (-2.0 * math.log(500000.0) / HEAD_SIZE)
    )
    angles = token_positions.astype(jnp.float32)[:, None] * inverse[None, :]
    cosine = jnp.cos(angles)[:, None, :]
    sine = jnp.sin(angles)[:, None, :]
    shaped = values.reshape(values.shape[0], heads, HEAD_SIZE)
    first = shaped[..., :half_dim]
    second = shaped[..., half_dim:]
    turned = jnp.concatenate(
        [first * cosine - second * sine, second * cosine + first * sine], axis=-1
    )
    return turned.reshape(values.shape[0], heads * HEAD_SIZE)


def shards(
    hidden,
    q_base,
    adapter_down,
    adapter_up,
    adapter_owner,
    turn_start,
    shard_lengths,
    stored_keys,
    stored_values,
    unrotated_turn_keys,
    incoming_values,
):
    holder = adapter_owner[0]
    slot_down = adapter_down[0]
    slot_up = adapter_up[0]
    got_down, got_up = (spread(slot_down, "ctx", holder), spread(slot_up, "ctx", holder))
    lowrank = jnp.dot(hidden, got_down, preferred_element_type=jnp.float32).astype(jnp.bfloat16)
    adapter_delta = jnp.dot(lowrank, got_up, preferred_element_type=jnp.float32)
    token_count = q_base.shape[0]
    slot_count = stored_keys.shape[0]
    shard_rows = token_count + slot_count
    ctx_size = lax.axis_size("ctx")
    myself = lax.axis_index("ctx")
    query_heads = q_base.shape[1] // HEAD_SIZE
    kv_heads = unrotated_turn_keys.shape[1] // HEAD_SIZE
    groups = query_heads // kv_heads
    local_tokens = jnp.arange(token_count, dtype=jnp.int32)
    token_positions = turn_start[0] + myself * token_count + local_tokens
    query_rows = apply_rotary(
        q_base.astype(jnp.float32) + 0.5 * adapter_delta, token_positions, query_heads
    ).astype(jnp.bfloat16)
    rotated_turn_keys = apply_rotary(
        unrotated_turn_keys.astype(jnp.float32), token_positions, kv_heads
    ).astype(jnp.bfloat16)
    grouped = query_rows.reshape(token_count, kv_heads, groups, HEAD_SIZE)
    key_here = jnp.concatenate([stored_keys, rotated_turn_keys], axis=0)
    value_here = jnp.concatenate([stored_values, incoming_values], axis=0)
    mine = myself * token_count + local_tokens
    score_scale = 1.0 / math.sqrt(HEAD_SIZE)
    shard_ids = jnp.arange(ctx_size, dtype=jnp.int32)

    def absorb(state, key_block, value_block, start):
        highest, denominator, accum = state
        row_count = key_block.shape[0]
        global_rows = start + jnp.arange(row_count, dtype=jnp.int32)
        owner_shard = global_rows // shard_rows
        within = global_rows % shard_rows
        is_cache = within < slot_count
        lengths_here = jnp.sum(
            jnp.where(owner_shard[:, None] == shard_ids[None, :], shard_lengths[None, :], 0), axis=1
        )
        token_number = owner_shard * token_count + (within - slot_count)
        allowed = jnp.where(
            is_cache[None, :],
            (within < lengths_here)[None, :],
            token_number[None, :] <= mine[:, None],
        )
        allowed = allowed[:, None, None, :]
        key_head_rows = key_block.reshape(-1, kv_heads, HEAD_SIZE)
        value_head_rows = value_block.reshape(-1, kv_heads, HEAD_SIZE)
        scores = (
            jnp.einsum("rhgd,khd->rhgk", grouped, key_head_rows, preferred_element_type=jnp.float32)
            * score_scale
        )
        new_high = jnp.maximum(highest, jnp.max(jnp.where(allowed, scores, -1e30), axis=-1))
        weights = jnp.where(allowed, jnp.exp(scores - new_high[..., None]), 0.0)
        fade = jnp.exp(highest - new_high)
        denominator = denominator * fade + jnp.sum(weights, axis=-1)
        product = jnp.einsum(
            "rhgk,khd->rhgd",
            weights.astype(jnp.bfloat16),
            value_head_rows,
            preferred_element_type=jnp.float32,
        )
        accum = accum * fade[..., None] + product
        return (new_high, denominator, accum)

    initial = (
        jnp.full((token_count, kv_heads, groups), -1e30, jnp.float32),
        jnp.zeros((token_count, kv_heads, groups), jnp.float32),
        jnp.zeros((token_count, kv_heads, groups, HEAD_SIZE), jnp.float32),
    )
    block_rows = shard_rows * 8

    def fold_pieces(state, pieces, start):
        key_piece, value_piece = pieces
        row_count = key_piece.shape[0]
        if row_count > block_rows and row_count % block_rows == 0:
            count = row_count // block_rows
            key_split = key_piece.reshape(count, block_rows, key_piece.shape[1])
            value_split = value_piece.reshape(count, block_rows, value_piece.shape[1])

            def inner(carry, items):
                key_one, value_one, number = items
                return (absorb(carry, key_one, value_one, start + number * block_rows), None)

            numbers = jnp.arange(count, dtype=jnp.int32)
            state, unused = lax.scan(inner, state, (key_split, value_split, numbers))
            return state
        return absorb(state, key_piece, value_piece, start)

    state = fold_pieces(
        initial,
        (
            lax.all_gather(key_here, "ctx", axis=0, tiled=True),
            lax.all_gather(value_here, "ctx", axis=0, tiled=True),
        ),
        jnp.int32(0),
    )
    highest, denominator, accum = state
    attended = accum / denominator[..., None]
    return attended.reshape(token_count, query_heads * HEAD_SIZE).astype(jnp.bfloat16)


def solution(mesh):
    return jax.shard_map(
        shards,
        mesh=mesh,
        in_specs=(
            P(("group", "ctx"), None),
            P(("group", "ctx"), "tp"),
            P(("group", "ctx"), None, None),
            P(("group", "ctx"), None, "tp"),
            P("group"),
            P("group"),
            P("group"),
            P(("group", "ctx"), "tp"),
            P(("group", "ctx"), "tp"),
            P(("group", "ctx"), "tp"),
            P(("group", "ctx"), "tp"),
        ),
        out_specs=P(("group", "ctx"), "tp"),
        check_vma=False,
    )
```

profile of v0, /device:TPU:0, one launch (start us, length us, event | category | flops | bytes accessed | tf_op | source)
XLA Modules:
  0.0 146.1 jit_solution(9558791827877660342)
XLA Ops:
  6.5 0.0 copy-start
  6.5 0.0 all-reduce.3.cloned.1.call-start
  7.3 0.0 copy-start.1
  7.3 3.1 %select_bitcast_fusion = bf16[16384,64]{0,1:T(8,128)(2,1)} fusion(bf16[1,16384,64]{1,2,0:T(8,128)(2,1)} %param.13, pred[]{:T(512)S(6)} %eq.22), kind=kLoop, calls=%fused_computation.2 | loop fusion | flops 1048576 | bytes 4194305 | tf_op jit(solution)/shard_map/jit(_where)/select_n | solution.py:12
  10.4 0.0 copy-done.1
  10.4 0.8 select_bitcast_fusion.1
  11.2 0.0 copy-start.5
  11.2 0.0 copy-start.3
  11.2 0.0 copy-start.4
  11.2 0.0 copy-start.6
  11.2 0.0 all-reduce.3.cloned.1.call-update
  11.2 0.0 copy-start.7
  11.3 0.0 copy-start.2
  12.0 0.0 copy-done.5
  12.0 0.1 multiply_cosine_fusion
  12.1 0.1 subtract_convert_fusion.1
  12.2 0.1 pad_maximum_fusion.3
  12.3 0.0 copy-done.3
  12.4 33.2 %all_gather.6 = bf16[640,256]{1,0:T(8,128)(2,1)S(1)} all-gather(bf16[80,256]{1,0:T(8,128)(2,1)S(1)} %pad_maximum_fusion.1), channel_id=1, replica_groups=mesh['group'=2,'ctx'=8,'tp'=2] {'ctx'}, dimensions={0}, use_global_device_ids=true | all-gather | bytes 368640 | tf_op jit(solution)/shard_map/all_gather | solution.py:137
  45.5 0.2 copy.39
  45.7 0.0 copy-done.4
  45.7 0.0 copy-done.6
  45.7 31.4 %all_gather.7 = bf16[640,256]{1,0:T(8,128)(2,1)S(1)} all-gather(bf16[80,256]{1,0:T(8,128)(2,1)S(1)} %pad_maximum_fusion.2), channel_id=1, replica_groups=mesh['group'=2,'ctx'=8,'tp'=2] {'ctx'}, dimensions={0}, use_global_device_ids=true | all-gather | bytes 368640 | tf_op jit(solution)/shard_map/all_gather | solution.py:138
  77.1 0.2 copy.42
  77.4 0.0 copy-done.7
  77.4 0.1 select_reduce_fusion.1
  77.5 0.1 compare_select_fusion
  77.6 56.6 %all-reduce.3.cloned.1.call-done = (bf16[64,4096]{1,0:T(8,128)(2,1)}, bf16[16384,64]{0,1:T(8,128)(2,1)}) async-done(((bf16[64,4096]{1,0:T(8,128)(2,1)}, bf16[16384,64]{0,1:T(8,128)(2,1)}), (bf16[64,4096]{1,0:T(8,128)(2,1)}, bf16[16384,64]{0,1:T(8,128)(2,1)})) %all-reduce.3.cloned.1.call-update) | async-done | bytes 2621456 | tf_op jit(solution)/shard_map/psum | solution.py:12
  134.2 0.0 copy-done
  134.2 0.0 copy-done.2
  134.2 2.6 %fusion.2 = f32[2,8,32,128]{3,1,2,0:T(8,128)S(1)} fusion(bf16[64,4096]{1,0:T(8,128)(2,1)} %get-tuple-element.5, bf16[16384,64]{0,1:T(8,128)(2,1)} %get-tuple-element.6, bf16[16,16384]{1,0:T(8,128)(2,1)S(1)} %copy-done, bf16[16,4096]{1,0:T(8,128)(2,1)S(1)} %copy-done.2), kind=kOutput, calls=%fused_computation.7 | convolution fusion | flops 42140672 | bytes 3538944 | tf_op jit(solution)/shard_map/dot_general | solution.py:50
  136.9 0.1 copy.52
  136.9 0.1 subtract_convert_fusion
  137.1 0.1 pad_maximum_fusion
  137.2 0.4 select_reduce_fusion
  137.6 0.4 fusion.6
  138.1 0.4 fusion.5
  138.5 0.7 copy.60
  (13 shorter events, 0.1 us)
Async XLA Ops:
  6.5 127.7 %copy-start = (bf16[16,16384]{1,0:T(8,128)(2,1)S(1)}, bf16[16,16384]{1,0:T(8,128)(2,1)}, u32[]{:S(2)}) copy-start(bf16[16,16384]{1,0:T(8,128)(2,1)} %param.11) | copy-start | bytes 1572868
  6.5 127.7 %all-reduce.3.cloned.1.call-start = ((), (), s32[]{:S(2)}) async-start(), calls=%async_computation | async-start | bytes 5242880 | tf_op jit(solution)/shard_map/psum | solution.py:12
  7.3 3.1 %copy-start.1 = (bf16[1,64,4096]{2,1,0:T(8,128)(2,1)S(1)}, bf16[1,64,4096]{2,1,0:T(8,128)(2,1)}, u32[]{:S(2)}) copy-start(bf16[1,64,4096]{2,1,0:T(8,128)(2,1)} %param.14) | copy-start | bytes 1572868
  11.2 0.8 copy-start.5
  11.2 1.1 copy-start.3
  11.2 34.5 %copy-start.4 = (bf16[64,256]{1,0:T(8,128)(2,1)S(1)}, bf16[64,256]{1,0:T(8,128)(2,1)}, u32[]{:S(2)}) copy-start(bf16[64,256]{1,0:T(8,128)(2,1)} %param.19) | copy-start | bytes 98308
  11.2 34.5 %copy-start.6 = (bf16[16,256]{1,0:T(8,128)(2,1)S(1)}, bf16[16,256]{1,0:T(8,128)(2,1)}, u32[]{:S(2)}) copy-start(bf16[16,256]{1,0:T(8,128)(2,1)} %param.21) | copy-start | bytes 24580
  11.2 66.2 %copy-start.7 = (s32[8]{0:T(128)S(1)}, s32[8]{0:T(128)}, u32[]{:S(2)}) copy-start(s32[8]{0:T(128)} %param.17) | copy-start | bytes 100
  11.3 123.0 %copy-start.2 = (bf16[16,4096]{1,0:T(8,128)(2,1)S(1)}, bf16[16,4096]{1,0:T(8,128)(2,1)}, u32[]{:S(2)}) copy-start(bf16[16,4096]{1,0:T(8,128)(2,1)} %param.12) | copy-start | bytes 393220
Sparse Core Ops, SparseCore 0:
  11.4 122.7 all-reduce.2
where the time goes:
time: 146 us
  blocking collectives  64.6 us (44%)
  waiting for transfers between devices  56.6 us (39%)
  between operations  15 us (10%)
  other arithmetic  5.13 us (4%)
  matrix products  3.5 us (2%)
    psum x1, waiting for transfers between devices, spread(): return lax.psum(jnp.where(mine, shard, jnp.zeros_like(shard)), axis)  56.6 us
    all_gather x1, blocking collectives, shards(): lax.all_gather(key_here, 'ctx', axis=0, tiled=True)  33.2 us
    all_gather x1, blocking collectives, shards(): lax.all_gather(value_here, 'ctx', axis=0, tiled=True)  31.4 us
    select_n x2, other arithmetic, spread(): return lax.psum(jnp.where(mine, shard, jnp.zeros_like(shard)), axis)  3.94 us
  transfers between devices with their start and end apart: 1, of which 1 were waited for; matrix products, arithmetic and copies ran while one was open for 1% of the time, Pallas kernels for 0%

commit v1 on v0

--- a/solution.py
+++ b/solution.py
@@ -9,7 +9,7 @@
 
 def spread(shard, axis, root):
     mine = lax.axis_index(axis) == root
-    return lax.psum(jnp.where(mine, shard, jnp.zeros_like(shard)), axis)
+    return jnp.sum(lax.all_gather(jnp.where(mine, shard, jnp.zeros_like(shard)), axis), axis=0)
 
 
 def apply_rotary(values, token_positions, heads):

time: 146 us -> 341 us (2.34)
  waiting for transfers between devices: 56.6 us -> 236 us
  other arithmetic: 5.13 us -> 18.8 us
    all_gather x0 -> x2, waiting for transfers between devices: none -> 236 us  [spread(): lax.all_gather(jnp.where(mine, shard, jnp.zeros_like(shard)), axis)]
    psum x1 -> x0, waiting for transfers between devices: 56.6 us -> none  [spread(): return lax.psum(jnp.where(mine, shard, jnp.zeros_like(shard)), axis)]
    reduce_sum x0 -> x2, other arithmetic: none -> 12.1 us  [spread(): jnp.sum(lax.all_gather(jnp.where(mine, shard, jnp.zeros_like(shard)), axi...]
  transfers between devices with their start and end apart: 1 -> 2, of which waited for: 1 -> 2; matrix products, arithmetic and copies ran while one was open for 1% -> 3% of each run, Pallas kernels for 0% -> 0%
where the time goes in v1:
time: 341 us
  waiting for transfers between devices  236 us (69%)
  blocking collectives  65.1 us (19%)
  other arithmetic  18.8 us (6%)
  between operations  15 us (4%)
  local copies, waits for them, and re-layouts  3.8 us (1%)
    all_gather x2, waiting for transfers between devices, spread(): lax.all_gather(jnp.where(mine, shard, jnp.zeros_like(shard)), axis)  236 us
    all_gather x1, blocking collectives, shards(): lax.all_gather(value_here, 'ctx', axis=0, tiled=True)  32.7 us
    all_gather x1, blocking collectives, shards(): lax.all_gather(key_here, 'ctx', axis=0, tiled=True)  32.4 us
    reduce_sum x2, other arithmetic, spread(): jnp.sum(lax.all_gather(jnp.where(mine, shard, jnp.zeros_like(shard)), axi...  12.1 us
  transfers between devices with their start and end apart: 2, of which 2 were waited for; matrix products, arithmetic and copies ran while one was open for 3% of the time, Pallas kernels for 0%

profile of v1, /device:TPU:0, one launch (start us, length us, event | category | flops | bytes accessed | tf_op | source)
XLA Modules:
  0.0 340.7 jit_solution(7169124188076441398)
XLA Ops:
  6.5 0.0 copy-start
  6.5 0.0 all-gather.5.cloned.1.call-start
  7.3 1.9 broadcast_select_fusion.1
  9.1 0.0 all-gather.5.cloned.1.call-update
  9.2 0.0 all-gather.3.cloned.1.call-start
  9.2 3.1 broadcast_select_fusion
  12.3 0.0 copy-start.7
  12.3 0.0 copy-start.5
  12.3 0.0 copy-start.6
  12.3 0.0 copy-start.8
  12.3 0.0 all-gather.3.cloned.1.call-update
  12.3 0.0 copy-start.9
  13.0 0.0 copy-done.7
  13.1 0.1 multiply_cosine_fusion
  13.2 0.1 subtract_convert_fusion.1
  13.3 0.1 pad_maximum_fusion.3
  13.4 0.0 copy-done.5
  13.4 32.4 %all_gather.14 = bf16[640,256]{1,0:T(8,128)(2,1)S(1)} all-gather(bf16[80,256]{1,0:T(8,128)(2,1)S(1)} %pad_maximum_fusion.1), channel_id=1, replica_groups=mesh['group'=2,'ctx'=8,'tp'=2] {'ctx'}, dimensions={0}, use_global_device_ids=true | all-gather | bytes 368640 | tf_op jit(solution)/shard_map/all_gather | solution.py:137
  45.8 0.9 copy.39
  46.7 0.0 copy-done.6
  46.7 0.0 copy-done.8
  46.7 32.7 %all_gather.17 = bf16[640,256]{1,0:T(8,128)(2,1)S(1)} all-gather(bf16[80,256]{1,0:T(8,128)(2,1)S(1)} %pad_maximum_fusion.2), channel_id=1, replica_groups=mesh['group'=2,'ctx'=8,'tp'=2] {'ctx'}, dimensions={0}, use_global_device_ids=true | all-gather | bytes 368640 | tf_op jit(solution)/shard_map/all_gather | solution.py:138
  79.4 0.9 copy.42
  80.3 0.0 copy-done.9
  80.3 0.1 select_reduce_fusion.1
  80.4 0.7 compare_select_fusion
  81.1 10.4 %all-gather.5.cloned.1.call-done = bf16[8,64,4096]{2,1,0:T(8,128)(2,1)} async-done(((bf16[1,64,4096]{2,1,0:T(8,128)(2,1)}), bf16[8,64,4096]{2,1,0:T(8,128)(2,1)}) %all-gather.5.cloned.1.call-update) | async-done | bytes 4194320 | tf_op jit(solution)/shard_map/all_gather | solution.py:12
  91.5 2.9 reduce_sum.44
  94.4 0.0 copy-start.3
  94.4 225.7 %all-gather.3.cloned.1.call-done = bf16[8,16384,64]{1,2,0:T(8,128)(2,1)} async-done(((bf16[1,16384,64]{1,2,0:T(8,128)(2,1)}), bf16[8,16384,64]{1,2,0:T(8,128)(2,1)}) %all-gather.3.cloned.1.call-update) | async-done | bytes 16777232 | tf_op jit(solution)/shard_map/all_gather | solution.py:12
  320.2 9.1 %reduce_sum.43 = bf16[16384,64]{0,1:T(8,128)(2,1)S(1)} reduce(bf16[8,16384,64]{1,2,0:T(8,128)(2,1)} %all-gather.3.cloned.1.call-done, bf16[]{:T(256)} %constant.49.clone.1), dimensions={0}, to_apply=%region_1.2 | reduce | flops 7340032 | bytes 18874370 | tf_op jit(solution)/shard_map/reduce_sum | solution.py:12
  329.3 0.0 copy-done
  329.3 0.0 copy-done.3
  329.3 1.0 fusion.2
  330.3 0.0 copy-start.2
  330.3 0.0 copy-start.4
  330.3 0.1 copy.52
  330.4 0.1 subtract_convert_fusion
  330.5 0.1 pad_maximum_fusion
  330.7 0.6 copy-done.2
  331.3 0.0 copy-done.4
  331.3 0.4 select_reduce_fusion
  331.7 0.0 copy-start.1
  331.7 0.4 fusion.6
  332.2 0.5 copy-done.1
  332.7 0.4 fusion.5
  333.1 0.7 copy.60
  (13 shorter events, 0.1 us)
Async XLA Ops:
  6.5 322.8 %copy-start = (bf16[16,16384]{1,0:T(8,128)(2,1)S(1)}, bf16[16,16384]{1,0:T(8,128)(2,1)}, u32[]{:S(2)}) copy-start(bf16[16,16384]{1,0:T(8,128)(2,1)} %param.11) | copy-start | bytes 1572868
  6.5 85.0 %all-gather.5.cloned.1.call-start = ((), (), s32[]{:S(2)}) async-start(), calls=%async_computation.1 | async-start | bytes 4718592 | tf_op jit(solution)/shard_map/all_gather | solution.py:12
  9.2 311.0 %all-gather.3.cloned.1.call-start = ((), (), s32[]{:S(2)}) async-start(), calls=%async_computation | async-start | bytes 18874368 | tf_op jit(solution)/shard_map/all_gather | solution.py:12
  12.3 0.7 copy-start.7
  12.3 1.1 copy-start.5
  12.3 34.4 %copy-start.6 = (bf16[64,256]{1,0:T(8,128)(2,1)S(1)}, bf16[64,256]{1,0:T(8,128)(2,1)}, u32[]{:S(2)}) copy-start(bf16[64,256]{1,0:T(8,128)(2,1)} %param.19) | copy-start | bytes 98308
  12.3 34.4 %copy-start.8 = (bf16[16,256]{1,0:T(8,128)(2,1)S(1)}, bf16[16,256]{1,0:T(8,128)(2,1)}, u32[]{:S(2)}) copy-start(bf16[16,256]{1,0:T(8,128)(2,1)} %param.21) | copy-start | bytes 24580
  12.3 68.0 %copy-start.9 = (s32[8]{0:T(128)S(1)}, s32[8]{0:T(128)}, u32[]{:S(2)}) copy-start(s32[8]{0:T(128)} %param.17) | copy-start | bytes 100
  94.4 234.9 %copy-start.3 = (bf16[16,4096]{1,0:T(8,128)(2,1)S(1)}, bf16[16,4096]{1,0:T(8,128)(2,1)}, u32[]{:S(2)}) copy-start(bf16[16,4096]{1,0:T(8,128)(2,1)} %param.12) | copy-start | bytes 393220
  330.3 1.0 copy-start.2
  330.3 1.0 copy-start.4
  331.7 1.0 copy-start.1
Sparse Core Ops, SparseCore 0:
  9.5 81.9 all-gather.4
  93.6 226.5 all-gather.2
